TPU v7x, 256 devices: a whole 4x4x8 slice. The times are simulated.
256 devices in a mesh: member: 8 (over z), cell: 32 (over x, y, core).
Axes of the slice: x: 4, y: 4, z: 8, core: 2. Of those that a mesh axis runs over, the one named last changes fastest.
Arguments:
- prior: float32 [64, 524288], P('member', 'cell')
- samples: float32 [64, 524288], P('member', 'cell')
- noise: float32 [2, 64, 524288], P(None, 'member', 'cell'), may hold values from -6 to 6
- obs_cells: int32 [2, 65536], P(None, 'cell'), may hold values from 0 to 524287, as said below
- obs_values: float32 [2, 65536], P(None, 'cell'), may hold values from -6 to 6
- seismic_mask: int32 [2, 4096], P(None, 'cell'), may hold values 0 or 1
Outputs:
- analysis: float32 [64, 524288], P('member', 'cell')
Inputs may be any that keep to these rules, and one draw needn't show every extreme that they name: obs_cells[s, o] lies in cells k * 16384 to (k + 1) * 16384 - 1 where k = o // 2048; cells may repeat.
All inputs are finite; a program needn't handle non-finite values. No bound on the sum of `seismic_mask` on one device may be relied on, other than what follows from the above.
Results may differ from a plain program's by a relative error of at most 0.0003.
Values sent between devices are 32-bit elements; how exact they have to be, the bound alone decides.
No kernel may reach another device: no remote copies, remote signals or barrier semaphores. Data moves between devices by JAX's collectives and lax.ppermute only.
A program may use at most 64 MiB of HBM per device.

v0:
```python
import math
import jax
import jax.numpy as jnp
from jax import lax
from jax.sharding import PartitionSpec as P

STEPS = 2


def advance(state, fresh, prior_slab, prior_part, precision_slab, target_slab, step, ncell):
    time_now = 0.6 - 0.1 * step
    alpha = 1.0 - 0.95 * time_now
    drift = -0.95 / alpha
    diffusion = 1.0 - 2.0 * drift * time_now
    cross_part = lax.dot_general(
        state,
        prior_slab,
        (((1,), (1,)), ((), ())),
        precision=lax.Precision.HIGHEST,
        preferred_element_type=jnp.float32,
    )
    cross, prior_sq = lax.psum((cross_part, prior_part), ("member", "cell"))
    dist = alpha * alpha * prior_sq[None, :] - 2.0 * alpha * cross
    weights = jax.nn.softmax(-dist / (2.0 * time_now * math.sqrt(ncell)), axis=1)
    mean = jnp.dot(
        weights, prior_slab, precision=lax.Precision.HIGHEST, preferred_element_type=jnp.float32
    )
    score = (alpha * mean - state) / time_now - (1.0 - time_now) * (
        precision_slab[None, :] * state - target_slab[None, :]
    )
    return state - 0.1 * (drift * state - diffusion * score) + math.sqrt(0.1 * diffusion) * fresh


def per_device(prior, samples, noise, obs_cells, obs_values, seismic_mask):
    cells = prior.shape[1]
    groups = lax.axis_size("member")
    width = cells // groups
    ncell = cells * lax.axis_size("cell")
    shard = lax.axis_index("cell")
    member_pos = lax.axis_index("member")
    local = obs_cells - shard * cells
    precision_field = jnp.zeros((cells,), jnp.float32)
    target_field = jnp.zeros((cells,), jnp.float32)
    for survey in range(obs_cells.shape[0]):
        where = local[survey]
        flags = seismic_mask[survey].astype(jnp.float32)
        weight = flags[where // 128]
        precision_field = precision_field.at[where].add(weight)
        target_field = target_field.at[where].add(weight * obs_values[survey])
    precision_slab = lax.dynamic_slice_in_dim(precision_field, member_pos * width, width)
    target_slab = lax.dynamic_slice_in_dim(target_field, member_pos * width, width)
    prior_slab = lax.all_to_all(prior, "member", split_axis=1, concat_axis=0, tiled=True)
    prior_part = jnp.sum(prior_slab * prior_slab, axis=1)
    state = samples
    for step in range(STEPS):
        slab, fresh = (
            lax.all_to_all(state, "member", split_axis=1, concat_axis=0, tiled=True),
            lax.all_to_all(noise[step], "member", split_axis=1, concat_axis=0, tiled=True),
        )
        slab = advance(
            slab, fresh, prior_slab, prior_part, precision_slab, target_slab, step, ncell
        )
        state = lax.all_to_all(slab, "member", split_axis=0, concat_axis=1, tiled=True)
    return state


def solution(mesh):
    in_specs = (
        P("member", "cell"),
        P("member", "cell"),
        P(None, "member", "cell"),
        P(None, "cell"),
        P(None, "cell"),
        P(None, "cell"),
    )
    out_specs = P("member", "cell")
    return jax.shard_map(
        per_device, mesh=mesh, in_specs=in_specs, out_specs=out_specs, check_vma=False
    )
```

profile of v0, /device:TPU:2, one launch (start us, length us, event | category | flops | bytes accessed | tf_op | source)
XLA Modules:
  0.0 346.3 jit_solution(6709701843080657037)
XLA Ops:
  0.0 8.6 %all-to-all-start.1 = ((f32[8,8,2048]{2,0,1:T(8,128)}), f32[8,8,2048]{2,0,1:T(8,128)S(1)}, u32[]{:S(2)}, u32[]{:S(2)}) async-start(f32[8,8,2048]{2,0,1:T(8,128)} %bitcast.90), calls=%async_computation.1 | async-start | bytes 1048576 | tf_op jit(solution)/shard_map/all_to_all | solution.py:52
  8.6 1.0 fusion.55
  9.7 16.4 %all-to-all-done.1 = f32[8,8,2048]{2,0,1:T(8,128)S(1)} async-done(((f32[8,8,2048]{2,0,1:T(8,128)}), f32[8,8,2048]{2,0,1:T(8,128)S(1)}, u32[]{:S(2)}, u32[]{:S(2)}) %all-to-all-start.1) | async-done | bytes 524320 | tf_op jit(solution)/shard_map/all_to_all | solution.py:52
  26.1 3.5 %all-to-all-start = ((f32[8,8,2048]{2,0,1:T(8,128)}), f32[8,8,2048]{2,0,1:T(8,128)S(1)}, u32[]{:S(2)}, u32[]{:S(2)}) async-start(f32[8,8,2048]{2,0,1:T(8,128)} %bitcast), calls=%async_computation | async-start | bytes 1048576 | tf_op jit(solution)/shard_map/all_to_all | solution.py:57
  29.7 0.7 copy-done.2
  30.4 17.0 %all-to-all-done = f32[8,8,2048]{2,0,1:T(8,128)S(1)} async-done(((f32[8,8,2048]{2,0,1:T(8,128)}), f32[8,8,2048]{2,0,1:T(8,128)S(1)}, u32[]{:S(2)}, u32[]{:S(2)}) %all-to-all-start) | async-done | bytes 524320 | tf_op jit(solution)/shard_map/all_to_all | solution.py:57
  47.5 3.6 %all-to-all-start.2 = ((f32[8,8,2048]{2,0,1:T(8,128)}), f32[8,8,2048]{2,0,1:T(8,128)S(1)}, u32[]{:S(2)}, u32[]{:S(2)}) async-start(f32[8,8,2048]{2,0,1:T(8,128)} %bitcast.17), calls=%async_computation.2 | async-start | bytes 1048576 | tf_op jit(solution)/shard_map/all_to_all | solution.py:58
  51.1 12.6 %gather_fusion = f32[2048]{0:T(1024)S(1)} fusion(f32[128]{0:T(128)S(1)} %get-tuple-element.16, s32[2048]{0:T(1024)S(1)} %broadcast_clamp_fusion.1), kind=kCustom, calls=%fused_computation | custom fusion | bytes 24576 | tf_op jit(solution)/shard_map/gather | solution.py:47
  63.8 11.3 %scatter_custom_fusion = f32[16384]{0:T(1024)S(1)} fusion(s32[2048]{0:T(1024)S(1)} %bitcast.97, f32[2048]{0:T(1024)S(1)} %gather_fusion, f32[]{:T(128)} %constant.33.clone.1), kind=kCustom, calls=%fused_computation.51 | custom fusion | flops 2048 | bytes 65540 | tf_op jit(solution)/shard_map/scatter-add | solution.py:48
  75.0 11.3 %scatter_custom_fusion.2 = f32[16384]{0:T(1024)S(1)} fusion(s32[2048]{0:T(1024)S(1)} %bitcast.98, f32[2048]{0:T(1024)S(1)} %mul.145, f32[]{:T(128)} %constant.33.clone.1), kind=kCustom, calls=%fused_computation.49 | custom fusion | flops 2048 | bytes 65540 | tf_op jit(solution)/shard_map/scatter-add | solution.py:49
  86.3 12.6 %gather_fusion.1 = f32[2048]{0:T(1024)S(1)} fusion(f32[128]{0:T(128)S(1)} %get-tuple-element.15, s32[2048]{0:T(1024)S(1)} %broadcast_clamp_fusion), kind=kCustom, calls=%fused_computation.1 | custom fusion | bytes 24576 | tf_op jit(solution)/shard_map/gather | solution.py:47
  99.0 11.6 %scatter_fusion = f32[16384]{0:T(1024)S(1)} fusion(f32[16384]{0:T(1024)S(1)} %scatter_custom_fusion, s32[2048]{0:T(1024)S(1)} %bitcast.91, f32[2048]{0:T(1024)S(1)} %gather_fusion.1), kind=kCustom, calls=%fused_computation.3 | custom fusion | flops 2048 | bytes 32768 | tf_op jit(solution)/shard_map/scatter-add | solution.py:48
  110.5 11.6 %scatter_fusion.1 = f32[16384]{0:T(1024)S(1)} fusion(f32[16384]{0:T(1024)S(1)} %scatter_custom_fusion.2, s32[2048]{0:T(1024)S(1)} %bitcast.92, f32[2048]{0:T(1024)S(1)} %mul.146), kind=kCustom, calls=%fused_computation.5 | custom fusion | flops 2048 | bytes 32768 | tf_op jit(solution)/shard_map/scatter-add | solution.py:49
  122.4 0.6 fusion.22
  122.9 76.2 %all-reduce = (f32[64,64]{1,0:T(8,128)S(1)}, f32[64]{0:T(128)S(1)}) all-reduce(f32[64,64]{1,0:T(8,128)S(1)} %fusion.22, f32[64]{0:T(128)S(1)} %reduce_sum.30), channel_id=1, replica_groups=mesh['member'=8,'cell'=32] {'member','cell'}, use_global_device_ids=true, to_apply=%region_2.3 | all-reduce | flops 4160 | bytes 33280 | tf_op jit(solution)/shard_map/psum | solution.py:22
  199.5 0.9 fusion.17
  200.3 23.0 %all_to_all.115 = f32[8,8,2048]{2,1,0:T(8,128)S(1)} all-to-all(f32[8,8,2048]{2,1,0:T(8,128)S(1)} %fusion.17), channel_id=1, replica_groups=mesh['member'=8,'cell'=32] {'member'}, dimensions={0} | all-to-all | bytes 1048576 | tf_op jit(solution)/shard_map/all_to_all | solution.py:63
  223.3 18.4 %all_to_all.116 = f32[8,8,2048]{2,0,1:T(8,128)S(1)} all-to-all(f32[8,8,2048]{2,0,1:T(8,128)S(1)} %bitcast.88), channel_id=1, replica_groups=mesh['member'=8,'cell'=32] {'member'}, dimensions={1} | all-to-all | bytes 1048576 | tf_op jit(solution)/shard_map/all_to_all | solution.py:57
  241.8 3.5 %all-to-all-start.5 = ((f32[8,8,2048]{2,0,1:T(8,128)}), f32[8,8,2048]{2,0,1:T(8,128)S(1)}, u32[]{:S(2)}, u32[]{:S(2)}) async-start(f32[8,8,2048]{2,0,1:T(8,128)} %bitcast.26), calls=%async_computation.5 | async-start | bytes 1048576 | tf_op jit(solution)/shard_map/all_to_all | solution.py:58
  245.3 0.6 fusion.19
  245.8 75.5 %psum.26 = f32[64,64]{1,0:T(8,128)S(1)} all-reduce(f32[64,64]{1,0:T(8,128)S(1)} %fusion.19), channel_id=1, replica_groups=mesh['member'=8,'cell'=32] {'member','cell'}, use_global_device_ids=true, to_apply=%region_9.10 | all-reduce | flops 4096 | bytes 32768 | tf_op jit(solution)/shard_map/psum | solution.py:22
  321.6 0.9 fusion.15
  322.5 23.0 %all_to_all.117 = f32[8,8,2048]{2,1,0:T(8,128)S(1)} all-to-all(f32[8,8,2048]{2,1,0:T(8,128)S(1)} %fusion.15), channel_id=1, replica_groups=mesh['member'=8,'cell'=32] {'member'}, dimensions={0} | all-to-all | bytes 1048576 | tf_op jit(solution)/shard_map/all_to_all | solution.py:63
  345.5 0.8 copy.10
  (26 shorter events, 1.0 us)
Async XLA Ops:
  0.0 8.6 %copy-start = (f32[2,8,16384]{2,1,0:T(8,128)S(1)}, f32[2,8,16384]{2,1,0:T(8,128)}, u32[]{:S(2)}) copy-start(f32[2,8,16384]{2,1,0:T(8,128)} %param.8) | copy-start | bytes 3145732
  0.0 26.1 %all-to-all-start.1 = ((f32[8,8,2048]{2,0,1:T(8,128)}), f32[8,8,2048]{2,0,1:T(8,128)S(1)}, u32[]{:S(2)}, u32[]{:S(2)}) async-start(f32[8,8,2048]{2,0,1:T(8,128)} %bitcast.90), calls=%async_computation.1 | async-start | bytes 1048576 | tf_op jit(solution)/shard_map/all_to_all | solution.py:52
  8.6 1.0 copy-start.1
  26.1 21.4 %all-to-all-start = ((f32[8,8,2048]{2,0,1:T(8,128)}), f32[8,8,2048]{2,0,1:T(8,128)S(1)}, u32[]{:S(2)}, u32[]{:S(2)}) async-start(f32[8,8,2048]{2,0,1:T(8,128)} %bitcast), calls=%async_computation | async-start | bytes 1048576 | tf_op jit(solution)/shard_map/all_to_all | solution.py:57
  29.7 0.7 copy-start.2
  47.5 3.6 %copy-start.3 = (s32[2,128]{1,0:T(2,128)S(1)}, s32[2,128]{1,0:T(2,128)}, u32[]{:S(2)}) copy-start(s32[2,128]{1,0:T(2,128)} %param.11) | copy-start | bytes 3076
  47.5 152.0 %all-to-all-start.2 = ((f32[8,8,2048]{2,0,1:T(8,128)}), f32[8,8,2048]{2,0,1:T(8,128)S(1)}, u32[]{:S(2)}, u32[]{:S(2)}) async-start(f32[8,8,2048]{2,0,1:T(8,128)} %bitcast.17), calls=%async_computation.2 | async-start | bytes 1048576 | tf_op jit(solution)/shard_map/all_to_all | solution.py:58
  241.8 79.9 %all-to-all-start.5 = ((f32[8,8,2048]{2,0,1:T(8,128)}), f32[8,8,2048]{2,0,1:T(8,128)S(1)}, u32[]{:S(2)}, u32[]{:S(2)}) async-start(f32[8,8,2048]{2,0,1:T(8,128)} %bitcast.26), calls=%async_computation.5 | async-start | bytes 1048576 | tf_op jit(solution)/shard_map/all_to_all | solution.py:58
where the time goes:
time: 347 us; the launch traced here: 346 us
  blocking collectives  216 us (62%)
  other arithmetic  46.5 us (13%)
  waiting for transfers between devices  33.5 us (10%)
  local copies, waits for them, and re-layouts  27.9 us (8%)
  starting transfers between devices  19.2 us (6%)
    psum x2, blocking collectives, advance(): cross, prior_sq = lax.psum((cross_part, prior_part), ('member', 'cell'))  152 us
    all_to_all x2, blocking collectives, per_device(): lax.all_to_all(slab, 'member', split_axis=0, concat_axis=1, tiled=True)  46 us
    gather x2, local copies, waits for them, and re-layouts, per_device(): weight = flags[where // 128]  25.2 us
    scatter-add x2, other arithmetic, per_device(): target_field = target_field.at[where].add(weight * obs_values[survey])  22.8 us
    scatter-add x2, other arithmetic, per_device(): precision_field = precision_field.at[where].add(weight)  22.8 us
    all_to_all x1, blocking collectives, per_device(): lax.all_to_all(state, 'member', split_axis=1, concat_axis=0, tiled=True)  18.4 us
    all_to_all x1, waiting for transfers between devices, per_device(): lax.all_to_all(state, 'member', split_axis=1, concat_axis=0, tiled=True)  17 us
    all_to_all x1, waiting for transfers between devices, per_device(): lax.all_to_all(prior, 'member', split_axis=1, concat_axis=0, tiled=True)  16.4 us
  transfers between devices with their start and end apart: 4, of which 2 were waited for; matrix products, arithmetic and copies ran while one was open for 21% of the time, Pallas kernels for 0%

commit v1 on v0

--- a/solution.py
+++ b/solution.py
@@ -5,6 +5,22 @@
 from jax.sharding import PartitionSpec as P
 
 STEPS = 2
+
+
+def swapped_with_each(array, axis, split, join):
+    ways, here = (lax.axis_size(axis), lax.axis_index(axis))
+    width = array.shape[split] // ways
+    shape = list(array.shape)
+    shape[split] = width
+    height = shape[join]
+    shape[join] = height * ways
+    full = jnp.zeros(shape, array.dtype)
+    for mask in range(ways):
+        part = lax.dynamic_slice_in_dim(array, (here ^ mask) * width, width, axis=split)
+        if mask:
+            part = lax.ppermute(part, axis, [(d, d ^ mask) for d in range(ways)])
+        full = lax.dynamic_update_slice_in_dim(full, part, (here ^ mask) * height, axis=join)
+    return full
 
 
 def advance(state, fresh, prior_slab, prior_part, precision_slab, target_slab, step, ncell):
@@ -54,7 +70,7 @@
     state = samples
     for step in range(STEPS):
         slab, fresh = (
-            lax.all_to_all(state, "member", split_axis=1, concat_axis=0, tiled=True),
+            swapped_with_each(state, "member", 1, 0),
             lax.all_to_all(noise[step], "member", split_axis=1, concat_axis=0, tiled=True),
         )
         slab = advance(

time: 347 us -> 339 us (0.977)
  starting transfers between devices: 19.2 us -> 48.2 us
  blocking collectives: 216 us -> 196 us
  waiting for transfers between devices: 33.5 us -> 15.1 us
    ppermute x0 -> x14, starting transfers between devices: none -> 32.1 us  [swapped_with_each(): part = lax.ppermute(part, axis, [(d, d ^ mask) for d in range(ways)])]
    all_to_all x1 -> x0, blocking collectives: 18.4 us -> none  [per_device(): lax.all_to_all(state, 'member', split_axis=1, concat_axis=0, tiled=True)]
    all_to_all x1 -> x0, waiting for transfers between devices: 17 us -> none  [per_device(): lax.all_to_all(state, 'member', split_axis=1, concat_axis=0, tiled=True)]
    all_to_all x1, waiting for transfers between devices: 16.4 us -> 0.01 us  [per_device(): lax.all_to_all(prior, 'member', split_axis=1, concat_axis=0, tiled=True)]
    ppermute x0 -> x14, waiting for transfers between devices: none -> 15.1 us  [swapped_with_each(): part = lax.ppermute(part, axis, [(d, d ^ mask) for d in range(ways)])]
    all_to_all x1 -> x0, starting transfers between devices: 3.5 us -> none  [per_device(): lax.all_to_all(state, 'member', split_axis=1, concat_axis=0, tiled=True)]
  transfers between devices with their start and end apart: 4 -> 17, of which waited for: 2 -> 5; matrix products, arithmetic and copies ran while one was open for 21% -> 22% of each run, Pallas kernels for 0% -> 0%
where the time goes in v1:
time: 339 us; the launch traced here: 338 us
  blocking collectives  196 us (58%)
  starting transfers between devices  48.2 us (14%)
  other arithmetic  46.5 us (14%)
  local copies, waits for them, and re-layouts  29.8 us (9%)
  waiting for transfers between devices  15.1 us (4%)
    psum x2, blocking collectives, advance(): cross, prior_sq = lax.psum((cross_part, prior_part), ('member', 'cell'))  151 us
    all_to_all x2, blocking collectives, per_device(): lax.all_to_all(slab, 'member', split_axis=0, concat_axis=1, tiled=True)  44.6 us
    ppermute x14, starting transfers between devices, swapped_with_each(): part = lax.ppermute(part, axis, [(d, d ^ mask) for d in range(ways)])  32.1 us
    gather x2, local copies, waits for them, and re-layouts, per_device(): weight = flags[where // 128]  25.2 us
    scatter-add x2, other arithmetic, per_device(): precision_field = precision_field.at[where].add(weight)  22.8 us
    scatter-add x2, other arithmetic, per_device(): target_field = target_field.at[where].add(weight * obs_values[survey])  22.8 us
    ppermute x14, waiting for transfers between devices, swapped_with_each(): part = lax.ppermute(part, axis, [(d, d ^ mask) for d in range(ways)])  15.1 us
    all_to_all x2, starting transfers between devices, per_device(): lax.all_to_all(noise[step], 'member', split_axis=1, concat_axis=0, tiled=...  9.84 us
  transfers between devices with their start and end apart: 17, of which 5 were waited for; matrix products, arithmetic and copies ran while one was open for 22% of the time, Pallas kernels for 0%

profile of v1, /device:TPU:2, one launch (start us, length us, event | category | flops | bytes accessed | tf_op | source)
XLA Modules:
  0.0 338.5 jit_solution(87303157790968444)
XLA Ops:
  1.1 2.0 collective-permute-start
  3.1 3.3 collective-permute-start.1
  6.4 6.4 %collective-permute-start.3 = (f32[8,2048]{1,0:T(8,128)S(1)}, f32[8,2048]{1,0:T(8,128)S(1)}, u32[]{:S(2)}, u32[]{:S(2)}) collective-permute-start(f32[8,2048]{1,0:T(8,128)S(1)} %get-tuple-element.19), channel_id=1, source_target_pairs={{0,128},{32,160},{64,192},{96,224},{128,0},{160,32},{192,64},{224,... | collective-permute-start | bytes 196616 | tf_op jit(solution)/shard_map/ppermute | solution.py:21
  12.8 6.3 %all-to-all-start = ((f32[8,8,2048]{2,0,1:T(8,128)}), f32[8,8,2048]{2,0,1:T(8,128)S(1)}, u32[]{:S(2)}, u32[]{:S(2)}) async-start(f32[8,8,2048]{2,0,1:T(8,128)} %bitcast), calls=%async_computation | async-start | bytes 1048576 | tf_op jit(solution)/shard_map/all_to_all | solution.py:68
  21.7 12.6 %gather_fusion = f32[2048]{0:T(1024)S(1)} fusion(f32[128]{0:T(128)S(1)} %get-tuple-element.32, s32[2048]{0:T(1024)S(1)} %broadcast_clamp_fusion.1), kind=kCustom, calls=%fused_computation | custom fusion | bytes 24576 | tf_op jit(solution)/shard_map/gather | solution.py:63
  34.3 12.6 %gather_fusion.1 = f32[2048]{0:T(1024)S(1)} fusion(f32[128]{0:T(128)S(1)} %get-tuple-element.31, s32[2048]{0:T(1024)S(1)} %broadcast_clamp_fusion), kind=kCustom, calls=%fused_computation.1 | custom fusion | bytes 24576 | tf_op jit(solution)/shard_map/gather | solution.py:63
  46.9 11.3 %scatter_custom_fusion.2 = f32[16384]{0:T(1024)S(1)} fusion(s32[2048]{0:T(1024)S(1)} %bitcast.75, f32[2048]{0:T(1024)S(1)} %mul.222, f32[]{:T(128)} %constant.39.clone.1), kind=kCustom, calls=%fused_computation.35 | custom fusion | flops 2048 | bytes 65540 | tf_op jit(solution)/shard_map/scatter-add | solution.py:65
  58.2 11.6 %scatter_fusion.1 = f32[16384]{0:T(1024)S(1)} fusion(f32[16384]{0:T(1024)S(1)} %scatter_custom_fusion.2, s32[2048]{0:T(1024)S(1)} %bitcast.69, f32[2048]{0:T(1024)S(1)} %mul.223), kind=kCustom, calls=%fused_computation.5 | custom fusion | flops 2048 | bytes 32768 | tf_op jit(solution)/shard_map/scatter-add | solution.py:65
  69.8 11.3 %scatter_custom_fusion = f32[16384]{0:T(1024)S(1)} fusion(s32[2048]{0:T(1024)S(1)} %bitcast.76, f32[2048]{0:T(1024)S(1)} %gather_fusion, f32[]{:T(128)} %constant.39.clone.1), kind=kCustom, calls=%fused_computation.37 | custom fusion | flops 2048 | bytes 65540 | tf_op jit(solution)/shard_map/scatter-add | solution.py:64
  81.1 11.6 %scatter_fusion = f32[16384]{0:T(1024)S(1)} fusion(f32[16384]{0:T(1024)S(1)} %scatter_custom_fusion, s32[2048]{0:T(1024)S(1)} %bitcast.70, f32[2048]{0:T(1024)S(1)} %gather_fusion.1), kind=kCustom, calls=%fused_computation.3 | custom fusion | flops 2048 | bytes 32768 | tf_op jit(solution)/shard_map/scatter-add | solution.py:64
  92.7 4.2 %collective-permute-start.5 = (f32[8,2048]{1,0:T(8,128)S(1)}, f32[8,2048]{1,0:T(8,128)S(1)}, u32[]{:S(2)}, u32[]{:S(2)}) collective-permute-start(f32[8,2048]{1,0:T(8,128)S(1)} %get-tuple-element.24), channel_id=1, source_target_pairs={{0,192},{32,224},{64,128},{96,160},{128,64},{160,96},{192,0},{224,... | collective-permute-start | bytes 196616 | tf_op jit(solution)/shard_map/ppermute | solution.py:21
  97.7 2.4 collective-permute-done.5
  100.2 6.4 %all-to-all-start.1 = ((f32[8,8,2048]{2,0,1:T(8,128)}), f32[8,8,2048]{2,0,1:T(8,128)S(1)}, u32[]{:S(2)}, u32[]{:S(2)}) async-start(f32[8,8,2048]{2,0,1:T(8,128)} %bitcast.13), calls=%async_computation.1 | async-start | bytes 1048576 | tf_op jit(solution)/shard_map/all_to_all | solution.py:74
  107.3 76.6 %all-reduce = (f32[64,64]{1,0:T(8,128)S(1)}, f32[64]{0:T(128)S(1)}) all-reduce(f32[64,64]{1,0:T(8,128)S(1)} %fusion.14, f32[64]{0:T(128)S(1)} %reduce_sum.30), channel_id=1, replica_groups=mesh['member'=8,'cell'=32] {'member','cell'}, use_global_device_ids=true, to_apply=%region_2.3 | all-reduce | flops 4160 | bytes 33280 | tf_op jit(solution)/shard_map/psum | solution.py:38
  185.1 23.0 %all_to_all.83 = f32[8,8,2048]{2,1,0:T(8,128)S(1)} all-to-all(f32[8,8,2048]{2,1,0:T(8,128)S(1)} %fusion.9), channel_id=1, replica_groups=mesh['member'=8,'cell'=32] {'member'}, dimensions={0} | all-to-all | bytes 1048576 | tf_op jit(solution)/shard_map/all_to_all | solution.py:79
  208.9 3.5 %all-to-all-start.3 = ((f32[8,8,2048]{2,0,1:T(8,128)}), f32[8,8,2048]{2,0,1:T(8,128)S(1)}, u32[]{:S(2)}, u32[]{:S(2)}) async-start(f32[8,8,2048]{2,0,1:T(8,128)} %bitcast.21), calls=%async_computation.3 | async-start | bytes 1048576 | tf_op jit(solution)/shard_map/all_to_all | solution.py:74
  212.4 2.8 collective-permute-start.8
  216.7 4.5 %collective-permute-start.10 = (f32[8,2048]{1,0:T(8,128)S(1)}, f32[8,2048]{1,0:T(8,128)S(1)}, u32[]{:S(2)}, u32[]{:S(2)}) collective-permute-start(f32[8,2048]{1,0:T(8,128)S(1)} %get-tuple-element.12), channel_id=1, source_target_pairs={{0,128},{32,160},{64,192},{96,224},{128,0},{160,32},{192,64},{224,... | collective-permute-start | bytes 196616 | tf_op jit(solution)/shard_map/ppermute | solution.py:21
  221.2 4.1 %collective-permute-start.12 = (f32[8,2048]{1,0:T(8,128)S(1)}, f32[8,2048]{1,0:T(8,128)S(1)}, u32[]{:S(2)}, u32[]{:S(2)}) collective-permute-start(f32[8,2048]{1,0:T(8,128)S(1)} %get-tuple-element.10), channel_id=1, source_target_pairs={{0,192},{32,224},{64,128},{96,160},{128,64},{160,96},{192,0},{224,... | collective-permute-start | bytes 196616 | tf_op jit(solution)/shard_map/ppermute | solution.py:21
  225.3 9.2 %collective-permute-done.8 = f32[8,2048]{1,0:T(8,128)S(1)} collective-permute-done((f32[8,2048]{1,0:T(8,128)S(1)}, f32[8,2048]{1,0:T(8,128)S(1)}, u32[]{:S(2)}, u32[]{:S(2)}) %collective-permute-start.8) | collective-permute-done | bytes 65568 | tf_op jit(solution)/shard_map/ppermute | solution.py:21
  234.6 2.0 collective-permute-start.13
  238.1 1.9 collective-permute-done.13
  240.6 74.3 %psum.26 = f32[64,64]{1,0:T(8,128)S(1)} all-reduce(f32[64,64]{1,0:T(8,128)S(1)} %fusion.11), channel_id=1, replica_groups=mesh['member'=8,'cell'=32] {'member','cell'}, use_global_device_ids=true, to_apply=%region_9.10 | all-reduce | flops 4096 | bytes 32768 | tf_op jit(solution)/shard_map/psum | solution.py:38
  316.1 21.6 %all_to_all.84 = f32[8,8,2048]{2,1,0:T(8,128)S(1)} all-to-all(f32[8,8,2048]{2,1,0:T(8,128)S(1)} %fusion.8), channel_id=1, replica_groups=mesh['member'=8,'cell'=32] {'member'}, dimensions={0} | all-to-all | bytes 1048576 | tf_op jit(solution)/shard_map/all_to_all | solution.py:79
  (71 shorter events, 12.6 us)
Async XLA Ops:
  0.0 1.0 copy-start.1
  1.0 18.0 %copy-start = (f32[2,8,16384]{2,1,0:T(8,128)S(1)}, f32[2,8,16384]{2,1,0:T(8,128)}, u32[]{:S(2)}) copy-start(f32[2,8,16384]{2,1,0:T(8,128)} %param.8) | copy-start | bytes 3145732
  1.1 91.6 %collective-permute-start = (f32[8,2048]{1,0:T(8,128)S(1)}, f32[8,2048]{1,0:T(8,128)S(1)}, u32[]{:S(2)}, u32[]{:S(2)}) collective-permute-start(f32[8,2048]{1,0:T(8,128)S(1)} %get-tuple-element.22), channel_id=1, source_target_pairs={{0,32},{32,0},{64,96},{96,64},{128,160},{160,128},{192,224},{224,1... | collective-permute-start | bytes 196616 | tf_op jit(solution)/shard_map/ppermute | solution.py:21
  3.1 93.8 %collective-permute-start.1 = (f32[8,2048]{1,0:T(8,128)S(1)}, f32[8,2048]{1,0:T(8,128)S(1)}, u32[]{:S(2)}, u32[]{:S(2)}) collective-permute-start(f32[8,2048]{1,0:T(8,128)S(1)} %get-tuple-element.21), channel_id=1, source_target_pairs={{0,64},{32,96},{64,0},{96,32},{128,192},{160,224},{192,128},{224,1... | collective-permute-start | bytes 196616 | tf_op jit(solution)/shard_map/ppermute | solution.py:21
  6.4 91.2 %collective-permute-start.2 = (f32[8,2048]{1,0:T(8,128)S(1)}, f32[8,2048]{1,0:T(8,128)S(1)}, u32[]{:S(2)}, u32[]{:S(2)}) collective-permute-start(f32[8,2048]{1,0:T(8,128)S(1)} %get-tuple-element.20), channel_id=1, source_target_pairs={{0,96},{32,64},{64,32},{96,0},{128,224},{160,192},{192,160},{224,1... | collective-permute-start | bytes 196616 | tf_op jit(solution)/shard_map/ppermute | solution.py:21
  6.4 91.3 %collective-permute-start.3 = (f32[8,2048]{1,0:T(8,128)S(1)}, f32[8,2048]{1,0:T(8,128)S(1)}, u32[]{:S(2)}, u32[]{:S(2)}) collective-permute-start(f32[8,2048]{1,0:T(8,128)S(1)} %get-tuple-element.19), channel_id=1, source_target_pairs={{0,128},{32,160},{64,192},{96,224},{128,0},{160,32},{192,64},{224,... | collective-permute-start | bytes 196616 | tf_op jit(solution)/shard_map/ppermute | solution.py:21
  12.8 84.9 %collective-permute-start.4 = (f32[8,2048]{1,0:T(8,128)S(1)}, f32[8,2048]{1,0:T(8,128)S(1)}, u32[]{:S(2)}, u32[]{:S(2)}) collective-permute-start(f32[8,2048]{1,0:T(8,128)S(1)} %get-tuple-element.18), channel_id=1, source_target_pairs={{0,160},{32,128},{64,224},{96,192},{128,32},{160,0},{192,96},{224,... | collective-permute-start | bytes 196616 | tf_op jit(solution)/shard_map/ppermute | solution.py:21
  12.8 87.4 %all-to-all-start = ((f32[8,8,2048]{2,0,1:T(8,128)}), f32[8,8,2048]{2,0,1:T(8,128)S(1)}, u32[]{:S(2)}, u32[]{:S(2)}) async-start(f32[8,8,2048]{2,0,1:T(8,128)} %bitcast), calls=%async_computation | async-start | bytes 1048576 | tf_op jit(solution)/shard_map/all_to_all | solution.py:68
  19.1 1.0 copy-start.2
  20.2 0.7 copy-start.3
  21.0 0.7 copy-start.4
  92.7 7.4 %collective-permute-start.5 = (f32[8,2048]{1,0:T(8,128)S(1)}, f32[8,2048]{1,0:T(8,128)S(1)}, u32[]{:S(2)}, u32[]{:S(2)}) collective-permute-start(f32[8,2048]{1,0:T(8,128)S(1)} %get-tuple-element.24), channel_id=1, source_target_pairs={{0,192},{32,224},{64,128},{96,160},{128,64},{160,96},{192,0},{224,... | collective-permute-start | bytes 196616 | tf_op jit(solution)/shard_map/ppermute | solution.py:21
  96.9 9.6 %collective-permute-start.6 = (f32[8,2048]{1,0:T(8,128)S(1)}, f32[8,2048]{1,0:T(8,128)S(1)}, u32[]{:S(2)}, u32[]{:S(2)}) collective-permute-start(f32[8,2048]{1,0:T(8,128)S(1)} %get-tuple-element.17), channel_id=1, source_target_pairs={{0,224},{32,192},{64,160},{96,128},{128,96},{160,64},{192,32},{224... | collective-permute-start | bytes 196616 | tf_op jit(solution)/shard_map/ppermute | solution.py:21
  100.2 84.1 %all-to-all-start.1 = ((f32[8,8,2048]{2,0,1:T(8,128)}), f32[8,8,2048]{2,0,1:T(8,128)S(1)}, u32[]{:S(2)}, u32[]{:S(2)}) async-start(f32[8,8,2048]{2,0,1:T(8,128)} %bitcast.13), calls=%async_computation.1 | async-start | bytes 1048576 | tf_op jit(solution)/shard_map/all_to_all | solution.py:74
  208.2 12.9 %collective-permute-start.7 = (f32[8,2048]{1,0:T(8,128)S(1)}, f32[8,2048]{1,0:T(8,128)S(1)}, u32[]{:S(2)}, u32[]{:S(2)}) collective-permute-start(f32[8,2048]{1,0:T(8,128)S(1)} %get-tuple-element.15), channel_id=1, source_target_pairs={{0,32},{32,0},{64,96},{96,64},{128,160},{160,128},{192,224},{224,1... | collective-permute-start | bytes 196616 | tf_op jit(solution)/shard_map/ppermute | solution.py:21
  208.9 106.4 %all-to-all-start.3 = ((f32[8,8,2048]{2,0,1:T(8,128)}), f32[8,8,2048]{2,0,1:T(8,128)S(1)}, u32[]{:S(2)}, u32[]{:S(2)}) async-start(f32[8,8,2048]{2,0,1:T(8,128)} %bitcast.21), calls=%async_computation.3 | async-start | bytes 1048576 | tf_op jit(solution)/shard_map/all_to_all | solution.py:74
  212.4 22.2 %collective-permute-start.8 = (f32[8,2048]{1,0:T(8,128)S(1)}, f32[8,2048]{1,0:T(8,128)S(1)}, u32[]{:S(2)}, u32[]{:S(2)}) collective-permute-start(f32[8,2048]{1,0:T(8,128)S(1)} %get-tuple-element.14), channel_id=1, source_target_pairs={{0,64},{32,96},{64,0},{96,32},{128,192},{160,224},{192,128},{224,1... | collective-permute-start | bytes 196616 | tf_op jit(solution)/shard_map/ppermute | solution.py:21
  215.2 21.3 %collective-permute-start.9 = (f32[8,2048]{1,0:T(8,128)S(1)}, f32[8,2048]{1,0:T(8,128)S(1)}, u32[]{:S(2)}, u32[]{:S(2)}) collective-permute-start(f32[8,2048]{1,0:T(8,128)S(1)} %get-tuple-element.13), channel_id=1, source_target_pairs={{0,96},{32,64},{64,32},{96,0},{128,224},{160,192},{192,160},{224,1... | collective-permute-start | bytes 196616 | tf_op jit(solution)/shard_map/ppermute | solution.py:21
  216.7 20.2 %collective-permute-start.10 = (f32[8,2048]{1,0:T(8,128)S(1)}, f32[8,2048]{1,0:T(8,128)S(1)}, u32[]{:S(2)}, u32[]{:S(2)}) collective-permute-start(f32[8,2048]{1,0:T(8,128)S(1)} %get-tuple-element.12), channel_id=1, source_target_pairs={{0,128},{32,160},{64,192},{96,224},{128,0},{160,32},{192,64},{224,... | collective-permute-start | bytes 196616 | tf_op jit(solution)/shard_map/ppermute | solution.py:21
  221.2 16.9 %collective-permute-start.11 = (f32[8,2048]{1,0:T(8,128)S(1)}, f32[8,2048]{1,0:T(8,128)S(1)}, u32[]{:S(2)}, u32[]{:S(2)}) collective-permute-start(f32[8,2048]{1,0:T(8,128)S(1)} %get-tuple-element.11), channel_id=1, source_target_pairs={{0,160},{32,128},{64,224},{96,192},{128,32},{160,0},{192,96},{224,... | collective-permute-start | bytes 196616 | tf_op jit(solution)/shard_map/ppermute | solution.py:21
  221.2 16.9 %collective-permute-start.12 = (f32[8,2048]{1,0:T(8,128)S(1)}, f32[8,2048]{1,0:T(8,128)S(1)}, u32[]{:S(2)}, u32[]{:S(2)}) collective-permute-start(f32[8,2048]{1,0:T(8,128)S(1)} %get-tuple-element.10), channel_id=1, source_target_pairs={{0,192},{32,224},{64,128},{96,160},{128,64},{160,96},{192,0},{224,... | collective-permute-start | bytes 196616 | tf_op jit(solution)/shard_map/ppermute | solution.py:21
  234.6 5.5 %collective-permute-start.13 = (f32[8,2048]{1,0:T(8,128)S(1)}, f32[8,2048]{1,0:T(8,128)S(1)}, u32[]{:S(2)}, u32[]{:S(2)}) collective-permute-start(f32[8,2048]{1,0:T(8,128)S(1)} %get-tuple-element.9), channel_id=1, source_target_pairs={{0,224},{32,192},{64,160},{96,128},{128,96},{160,64},{192,32},{224... | collective-permute-start | bytes 196616 | tf_op jit(solution)/shard_map/ppermute | solution.py:21
